TPU v7x, 32 devices: a whole 2x2x4 slice. The times are simulated.
32 devices in a mesh: replica: 16 (over z, x, core), fsdp: 2 (over y).
Axes of the slice: x: 2, y: 2, z: 4, core: 2. Of those that a mesh axis runs over, the one named last changes fastest.
Arguments:
- block_in: bfloat16 [4096, 1024], P(('replica', 'fsdp')), may hold values from -6 to 6
- w_query: bfloat16 [1024, 2048], P('fsdp'), may hold values from -1 to 1
- key_projection: bfloat16 [1024, 1024], P('fsdp'), may hold values from -1 to 1
- value_projection: bfloat16 [1024, 1024], P('fsdp'), may hold values from -0.1875 to 0.1875
- w_out: bfloat16 [2048, 1024], P('fsdp'), may hold values from -0.5 to 0.5
- w_gate: bfloat16 [1024, 3072], P('fsdp'), may hold values from -0.1875 to 0.1875
- w_up: bfloat16 [1024, 3072], P('fsdp'), may hold values from -0.1875 to 0.1875
- w_down: bfloat16 [3072, 1024], P('fsdp'), may hold values from -0.109375 to 0.109375
- attn_gain: float32 [1024], replicated, may hold values from 0.5 to 1.5
- mlp_gain: float32 [1024], replicated, may hold values from 0.5 to 1.5
- query_gain: float32 [128], replicated, may hold values from 0.5 to 3.5
- key_norm_gain: float32 [128], replicated, may hold values from 0.5 to 3.5
- segment_ids: int32 [16, 256], P('replica'), may hold values from 0 to 2, as said below
- positions: int32 [4096], P(('replica', 'fsdp')), may hold values from 0 to 255, as said below
- cotangent: bfloat16 [4096, 1024], P(('replica', 'fsdp')), may hold values from -6 to 6
Outputs:
- block_out: bfloat16 [4096, 1024], P(('replica', 'fsdp'))
- d_block_in: float32 [4096, 1024], P(('replica', 'fsdp'))
- grad_query: float32 [1024, 2048], P('fsdp')
- grad_key: float32 [1024, 1024], P('fsdp')
- grad_value: float32 [1024, 1024], P('fsdp')
- grad_out: float32 [2048, 1024], P('fsdp')
- grad_gate: float32 [1024, 3072], P('fsdp')
- grad_up: float32 [1024, 3072], P('fsdp')
- grad_down: float32 [3072, 1024], P('fsdp')
- grad_attn_gain: float32 [1024], replicated
- grad_mlp_gain: float32 [1024], replicated
- grad_query_gain: float32 [128], replicated
- grad_key_gain: float32 [128], replicated
Inputs may be any that keep to these rules, and one draw needn't show every extreme that they name: `segment_ids`: in each sequence the document numbers start at 0 at its first token and rise by one at each new document, never falling; a sequence holds at most three documents, the first sequence a single one, every other sequence exactly three. `positions`: A token's position is its place within its document, counted from 0 at the document's first token.
All inputs are finite; a program needn't handle non-finite values.
Results may differ from a plain program's by a relative error of at most 0.02.
The roundings to bfloat16 on the way count: a program that leaves them out, or rounds other values in their place, can miss the bound.
Values may be sent and summed in bfloat16 or wider, within the bound.
No kernel may reach another device: no remote copies, remote signals or barrier semaphores. Data moves between devices by JAX's collectives and lax.ppermute only.
A program may use at most 192 MiB of HBM per device.

v0:
```python
import jax
import jax.numpy as jnp
from jax import lax
from jax.sharding import PartitionSpec as P

QUERY_HEADS = 16
KEY_VALUE_HEADS = 8
HEAD_SIZE = 128
EPS = 1e-06
THETA = 1000000.0
NEG = -1e30


def inv_rms(value):
    return lax.rsqrt(jnp.mean(value * value, axis=-1, keepdims=True) + EPS)


def norm_backward(grad, value, scale, gain):
    upstream = grad * gain
    return scale * (
        upstream - value * scale * scale * jnp.mean(upstream * value, axis=-1, keepdims=True)
    )


def rope_tables(position_row, width):
    half = width // 2
    freq = jnp.exp(
        -(jnp.arange(half, dtype=jnp.float32) * (2.0 / width)) * jnp.log(jnp.float32(THETA))
    )
    angle = position_row.astype(jnp.float32)[:, None] * freq[None, :]
    cos_tab = jnp.concatenate([jnp.cos(angle), jnp.cos(angle)], axis=-1)[:, None, :]
    sin_tab = jnp.concatenate([jnp.sin(angle), jnp.sin(angle)], axis=-1)[:, None, :]
    return (cos_tab, sin_tab)


def rotate(values_in):
    half = values_in.shape[-1] // 2
    return jnp.concatenate([-values_in[..., half:], values_in[..., :half]], axis=-1)


def rotate_back(values_in):
    half = values_in.shape[-1] // 2
    return jnp.concatenate([values_in[..., half:], -values_in[..., :half]], axis=-1)


def plain_product(left, right):
    return jnp.dot(left, right, preferred_element_type=jnp.float32)


def dot_right_t(left, right):
    return lax.dot_general(
        left, right, (((1,), (1,)), ((), ())), preferred_element_type=jnp.float32
    )


def rounded_partial(left, right):
    return lax.dot_general(
        left, right, (((0,), (0,)), ((), ())), preferred_element_type=jnp.bfloat16
    )


def attention_weights(w_query, key_projection, value_projection, w_out):
    return (
        lax.all_gather(w_query, "fsdp", axis=0, tiled=True),
        lax.all_gather(key_projection, "fsdp", axis=0, tiled=True),
        lax.all_gather(value_projection, "fsdp", axis=0, tiled=True),
        lax.all_gather(w_out, "fsdp", axis=0, tiled=True),
    )


def mlp_weights(w_gate, w_up, w_down):
    return (
        lax.all_gather(w_gate, "fsdp", axis=0, tiled=True),
        lax.all_gather(w_up, "fsdp", axis=0, tiled=True),
        lax.all_gather(w_down, "fsdp", axis=0, tiled=True),
    )


def context(k_rot, value_rows):
    return (
        lax.all_gather(k_rot, "fsdp", axis=0, tiled=True),
        lax.all_gather(value_rows, "fsdp", axis=0, tiled=True),
    )


def masked_scores(grouped_heads, keys_all, allowed):
    scores = jnp.einsum(
        "nkgd,mkd->kgnm", grouped_heads, keys_all, preferred_element_type=jnp.float32
    ) * HEAD_SIZE ** (-0.5)
    return jnp.where(allowed[None, None], scores, NEG)


def attend(query_rotated, keys_all, values_all, allowed):
    item_count = query_rotated.shape[0]
    grouped_heads = query_rotated.reshape(
        item_count, KEY_VALUE_HEADS, QUERY_HEADS // KEY_VALUE_HEADS, HEAD_SIZE
    )
    scores = masked_scores(grouped_heads, keys_all, allowed)
    top = jnp.max(scores, axis=-1, keepdims=True)
    lse = top + jnp.log(jnp.sum(jnp.exp(scores - top), axis=-1, keepdims=True))
    probs = jnp.exp(scores - lse).astype(jnp.bfloat16)
    mixed = jnp.einsum("kgnm,mkd->nkgd", probs, values_all, preferred_element_type=jnp.float32)
    return (mixed.astype(jnp.bfloat16).reshape(item_count, QUERY_HEADS * HEAD_SIZE), lse)


def attend_back(query_rotated, keys_all, values_all, allowed, lse, attention_gradient):
    item_count = query_rotated.shape[0]
    grouped_heads = query_rotated.reshape(
        item_count, KEY_VALUE_HEADS, QUERY_HEADS // KEY_VALUE_HEADS, HEAD_SIZE
    )
    grouped_gradient = attention_gradient.reshape(
        item_count, KEY_VALUE_HEADS, QUERY_HEADS // KEY_VALUE_HEADS, HEAD_SIZE
    )
    probs = jnp.exp(masked_scores(grouped_heads, keys_all, allowed) - lse)
    probs_b = probs.astype(jnp.bfloat16)
    d_prob = jnp.einsum(
        "nkgd,mkd->kgnm", grouped_gradient, values_all, preferred_element_type=jnp.float32
    )
    d_scores = (
        probs * (d_prob - jnp.sum(probs * d_prob, axis=-1, keepdims=True)) * HEAD_SIZE ** (-0.5)
    ).astype(jnp.bfloat16)
    d_qrot = jnp.einsum(
        "kgnm,mkd->nkgd", d_scores, keys_all, preferred_element_type=jnp.float32
    ).reshape(item_count, QUERY_HEADS, HEAD_SIZE)
    d_krot = jnp.einsum(
        "kgnm,nkgd->mkd", d_scores, grouped_heads, preferred_element_type=jnp.float32
    )
    values_gradient = jnp.einsum(
        "kgnm,nkgd->mkd", probs_b, grouped_gradient, preferred_element_type=jnp.float32
    )
    return (d_qrot, d_krot, values_gradient)


def shards(
    block_in,
    w_query,
    key_projection,
    value_projection,
    w_out,
    w_gate,
    w_up,
    w_down,
    attn_gain,
    mlp_gain,
    query_gain,
    key_norm_gain,
    segment_ids,
    positions,
    cotangent,
):
    item_count = block_in.shape[0]
    segment_row = segment_ids[0]
    sequence_length = segment_row.shape[0]
    offset = lax.axis_index("fsdp") * item_count
    local_segments = lax.dynamic_slice_in_dim(segment_row, offset, item_count)
    query_index = offset + jnp.arange(item_count, dtype=jnp.int32)
    key_index = jnp.arange(sequence_length, dtype=jnp.int32)
    allowed = (key_index[None, :] <= query_index[:, None]) & (
        segment_row[None, :] == local_segments[:, None]
    )
    resid = block_in.astype(jnp.float32)
    scale_one = inv_rms(resid)
    normed_rows = (resid * scale_one * attn_gain).astype(jnp.bfloat16)
    query_all, key_gathered, value_gathered, out_all = attention_weights(
        w_query, key_projection, value_projection, w_out
    )
    q_raw = plain_product(normed_rows, query_all).reshape(item_count, QUERY_HEADS, HEAD_SIZE)
    key_unnormed = plain_product(normed_rows, key_gathered).reshape(
        item_count, KEY_VALUE_HEADS, HEAD_SIZE
    )
    value_rows = (
        plain_product(normed_rows, value_gathered)
        .astype(jnp.bfloat16)
        .reshape(item_count, KEY_VALUE_HEADS, HEAD_SIZE)
    )
    q_scale = inv_rms(q_raw)
    key_scale = inv_rms(key_unnormed)
    q_normed = q_raw * q_scale * query_gain
    k_normed = key_unnormed * key_scale * key_norm_gain
    cos_tab, sin_tab = rope_tables(positions, HEAD_SIZE)
    query_rotated = (q_normed * cos_tab + rotate(q_normed) * sin_tab).astype(jnp.bfloat16)
    k_rot = (k_normed * cos_tab + rotate(k_normed) * sin_tab).astype(jnp.bfloat16)
    keys_all, values_all = context(k_rot, value_rows)
    attn_out, lse = attend(query_rotated, keys_all, values_all, allowed)
    mid = resid + plain_product(attn_out, out_all)
    scale_two = inv_rms(mid)
    normed_two = (mid * scale_two * mlp_gain).astype(jnp.bfloat16)
    gate_all, up_all, down_all = mlp_weights(w_gate, w_up, w_down)
    gate = plain_product(normed_two, gate_all)
    up = plain_product(normed_two, up_all)
    sig = jax.nn.sigmoid(gate)
    hidden = (gate * sig * up).astype(jnp.bfloat16)
    block_out = (mid + plain_product(hidden, down_all)).astype(jnp.bfloat16)
    back_gate, back_up, back_down = (gate_all, up_all, down_all)
    d_hidden = dot_right_t(cotangent, back_down)
    d_gate = (d_hidden * up * sig * (1.0 + gate * (1.0 - sig))).astype(jnp.bfloat16)
    d_up = (d_hidden * gate * sig).astype(jnp.bfloat16)
    grad_down = rounded_partial(hidden, cotangent)
    grad_gate = rounded_partial(normed_two, d_gate)
    grad_up = rounded_partial(normed_two, d_up)
    mlp_shards = (
        lax.psum_scatter(grad_gate, "fsdp", scatter_dimension=0, tiled=True).astype(jnp.float32),
        lax.psum_scatter(grad_up, "fsdp", scatter_dimension=0, tiled=True).astype(jnp.float32),
        lax.psum_scatter(grad_down, "fsdp", scatter_dimension=0, tiled=True).astype(jnp.float32),
    )
    d_normed_two = dot_right_t(d_gate, back_gate) + dot_right_t(d_up, back_up)
    grad_mlp_gain = jnp.sum(d_normed_two * mid * scale_two, axis=0)
    d_mid = cotangent.astype(jnp.float32) + norm_backward(d_normed_two, mid, scale_two, mlp_gain)
    d_mid_b = d_mid.astype(jnp.bfloat16)
    back_query, back_key, back_value, back_out = (query_all, key_gathered, value_gathered, out_all)
    back_keys, back_values = (keys_all, values_all)
    attention_gradient = dot_right_t(d_mid_b, back_out).astype(jnp.bfloat16)
    d_qrot, d_krot_all, d_values_all = attend_back(
        query_rotated, back_keys, back_values, allowed, lse, attention_gradient
    )
    d_krot, values_gradient = (
        lax.psum_scatter(
            d_krot_all.astype(jnp.bfloat16), "fsdp", scatter_dimension=0, tiled=True
        ).astype(jnp.float32),
        lax.psum_scatter(
            d_values_all.astype(jnp.bfloat16), "fsdp", scatter_dimension=0, tiled=True
        ).astype(jnp.float32),
    )
    d_qnormed = d_qrot * cos_tab + rotate_back(d_qrot * sin_tab)
    normed_key_gradient = d_krot * cos_tab + rotate_back(d_krot * sin_tab)
    grad_query_gain = jnp.sum(d_qnormed * q_raw * q_scale, axis=(0, 1))
    grad_key_gain = jnp.sum(normed_key_gradient * key_unnormed * key_scale, axis=(0, 1))
    d_query = (
        norm_backward(d_qnormed, q_raw, q_scale, query_gain)
        .astype(jnp.bfloat16)
        .reshape(item_count, QUERY_HEADS * HEAD_SIZE)
    )
    key_gradient = (
        norm_backward(normed_key_gradient, key_unnormed, key_scale, key_norm_gain)
        .astype(jnp.bfloat16)
        .reshape(item_count, KEY_VALUE_HEADS * HEAD_SIZE)
    )
    value_gradient = values_gradient.astype(jnp.bfloat16).reshape(
        item_count, KEY_VALUE_HEADS * HEAD_SIZE
    )
    grad_out = rounded_partial(attn_out, d_mid_b)
    grad_query = rounded_partial(normed_rows, d_query)
    grad_key = rounded_partial(normed_rows, key_gradient)
    grad_value = rounded_partial(normed_rows, value_gradient)
    attn_shards = (
        lax.psum_scatter(grad_query, "fsdp", scatter_dimension=0, tiled=True).astype(jnp.float32),
        lax.psum_scatter(grad_key, "fsdp", scatter_dimension=0, tiled=True).astype(jnp.float32),
        lax.psum_scatter(grad_value, "fsdp", scatter_dimension=0, tiled=True).astype(jnp.float32),
        lax.psum_scatter(grad_out, "fsdp", scatter_dimension=0, tiled=True).astype(jnp.float32),
    )
    d_normed = (
        dot_right_t(d_query, back_query)
        + dot_right_t(key_gradient, back_key)
        + dot_right_t(value_gradient, back_value)
    )
    grad_attn_gain = jnp.sum(d_normed * resid * scale_one, axis=0)
    d_block_in = d_mid + norm_backward(d_normed, resid, scale_one, attn_gain)
    gains = lax.psum(
        (grad_attn_gain, grad_mlp_gain, grad_query_gain, grad_key_gain), ("replica", "fsdp")
    )
    totals = (
        lax.psum(attn_shards[0].astype(jnp.bfloat16), "replica").astype(jnp.float32),
        lax.psum(attn_shards[1].astype(jnp.bfloat16), "replica").astype(jnp.float32),
        lax.psum(attn_shards[2].astype(jnp.bfloat16), "replica").astype(jnp.float32),
        lax.psum(attn_shards[3].astype(jnp.bfloat16), "replica").astype(jnp.float32),
        lax.psum(mlp_shards[0].astype(jnp.bfloat16), "replica").astype(jnp.float32),
        lax.psum(mlp_shards[1].astype(jnp.bfloat16), "replica").astype(jnp.float32),
        lax.psum(mlp_shards[2].astype(jnp.bfloat16), "replica").astype(jnp.float32),
    )
    return (
        block_out,
        d_block_in,
        totals[0],
        totals[1],
        totals[2],
        totals[3],
        totals[4],
        totals[5],
        totals[6],
        gains[0],
        gains[1],
        gains[2],
        gains[3],
    )


def solution(mesh):
    in_specs = (
        P(("replica", "fsdp"), None),
        P("fsdp", None),
        P("fsdp", None),
        P("fsdp", None),
        P("fsdp", None),
        P("fsdp", None),
        P("fsdp", None),
        P("fsdp", None),
        P(),
        P(),
        P(),
        P(),
        P("replica", None),
        P(("replica", "fsdp")),
        P(("replica", "fsdp"), None),
    )
    out_specs = (
        P(("replica", "fsdp"), None),
        P(("replica", "fsdp"), None),
        P("fsdp", None),
        P("fsdp", None),
        P("fsdp", None),
        P("fsdp", None),
        P("fsdp", None),
        P("fsdp", None),
        P("fsdp", None),
        P(),
        P(),
        P(),
        P(),
    )
    return jax.shard_map(shards, mesh=mesh, in_specs=in_specs, out_specs=out_specs, check_vma=False)
```

profile of v0, /device:TPU:0, one launch (start us, length us, event | category | flops | bytes accessed | tf_op | source)
XLA Modules:
  0.0 1245.7 jit_solution(10393132843414137143)
XLA Ops:
  13.5 31.9 %all-gather.10.cloned.1.call-done = bf16[1024,1024]{1,0:T(8,128)(2,1)} async-done(((bf16[512,1024]{1,0:T(8,128)(2,1)}), bf16[1024,1024]{1,0:T(8,128)(2,1)}) %all-gather.10.cloned.1.call-update) | async-done | bytes 2097168 | tf_op jit(solution)/shard_map/all_gather | solution.py:65
  47.9 32.2 %all-gather.8.cloned.1.call-done = bf16[1024,1024]{1,0:T(8,128)(2,1)} async-done(((bf16[512,1024]{1,0:T(8,128)(2,1)}), bf16[1024,1024]{1,0:T(8,128)(2,1)}) %all-gather.8.cloned.1.call-update) | async-done | bytes 2097168 | tf_op jit(solution)/shard_map/all_gather | solution.py:66
  83.1 8.7 all_gather.30
  91.8 15.3 %all_gather.28 = bf16[256,8,128]{0,2,1:T(8,128)(2,1)} all-gather(bf16[128,8,128]{0,2,1:T(8,128)(2,1)S(1)} %bitcast.203), channel_id=1, replica_groups=mesh['replica'=16,'fsdp'=2] {'fsdp'}, dimensions={0}, use_global_device_ids=true | all-gather | bytes 786432 | tf_op jit(solution)/shard_map/all_gather | solution.py:82
  107.1 36.9 %all-gather.12.cloned.1.call-done = bf16[1024,2048]{1,0:T(8,128)(2,1)} async-done(((bf16[512,2048]{1,0:T(8,128)(2,1)}), bf16[1024,2048]{1,0:T(8,128)(2,1)}) %all-gather.12.cloned.1.call-update) | async-done | bytes 4194320 | tf_op jit(solution)/shard_map/all_gather | solution.py:64
  151.7 50.5 %all-gather.14.cloned.1.call-done = bf16[2048,1024]{1,0:T(8,128)(2,1)} async-done(((bf16[1024,1024]{1,0:T(8,128)(2,1)}), bf16[2048,1024]{1,0:T(8,128)(2,1)}) %all-gather.14.cloned.1.call-update) | async-done | bytes 4194320 | tf_op jit(solution)/shard_map/all_gather | solution.py:67
  206.9 77.0 %all-gather.16.cloned.1.call-done = bf16[1024,3072]{1,0:T(8,128)(2,1)} async-done(((bf16[512,3072]{1,0:T(8,128)(2,1)}), bf16[1024,3072]{1,0:T(8,128)(2,1)}) %all-gather.16.cloned.1.call-update) | async-done | bytes 6291472 | tf_op jit(solution)/shard_map/all_gather | solution.py:73
  283.9 5.0 fusion.78
  288.9 76.8 %all-gather.18.cloned.1.call-done = bf16[1024,3072]{1,0:T(8,128)(2,1)} async-done(((bf16[512,3072]{1,0:T(8,128)(2,1)}), bf16[1024,3072]{1,0:T(8,128)(2,1)}) %all-gather.18.cloned.1.call-update) | async-done | bytes 6291472 | tf_op jit(solution)/shard_map/all_gather | solution.py:74
  365.7 5.0 fusion.79
  370.7 76.9 %all-gather.20.cloned.1.call-done = bf16[3072,1024]{1,0:T(8,128)(2,1)} async-done(((bf16[1536,1024]{1,0:T(8,128)(2,1)}), bf16[3072,1024]{1,0:T(8,128)(2,1)}) %all-gather.20.cloned.1.call-update) | async-done | bytes 6291472 | tf_op jit(solution)/shard_map/all_gather | solution.py:75
  447.6 7.1 multiply_convert_fusion
  454.8 5.6 fusion.80
  480.4 10.3 reduce-scatter.12.cloned.1.call-done
  498.9 9.3 reduce-scatter.28.cloned.1.call-done
  557.7 19.3 %reduce-scatter.18.cloned.1.call-done = bf16[512,1024]{1,0:T(8,128)(2,1)} async-done(((bf16[1024,1024]{1,0:T(8,128)(2,1)}), bf16[512,1024]{1,0:T(8,128)(2,1)}) %reduce-scatter.18.cloned.1.call-update) | async-done | bytes 1048592 | tf_op jit(solution)/shard_map/reduce_scatter | solution.py:248
  577.0 57.1 %reduce-scatter.14.cloned.1.call-done = bf16[512,2048]{1,0:T(8,128)(2,1)} async-done(((bf16[1024,2048]{1,0:T(8,128)(2,1)}), bf16[512,2048]{1,0:T(8,128)(2,1)}) %reduce-scatter.14.cloned.1.call-update) | async-done | bytes 2097168 | tf_op jit(solution)/shard_map/reduce_scatter | solution.py:246
  634.1 57.3 %reduce-scatter.20.cloned.1.call-done = bf16[1024,1024]{1,0:T(8,128)(2,1)} async-done(((bf16[2048,1024]{1,0:T(8,128)(2,1)}), bf16[1024,1024]{1,0:T(8,128)(2,1)}) %reduce-scatter.20.cloned.1.call-update) | async-done | bytes 2097168 | tf_op jit(solution)/shard_map/reduce_scatter | solution.py:249
  691.4 79.9 %reduce-scatter.22.cloned.1.call-done = bf16[512,3072]{1,0:T(8,128)(2,1)} async-done(((bf16[1024,3072]{1,0:T(8,128)(2,1)}), bf16[512,3072]{1,0:T(8,128)(2,1)}) %reduce-scatter.22.cloned.1.call-update) | async-done | bytes 3145744 | tf_op jit(solution)/shard_map/reduce_scatter | solution.py:202
  771.3 79.9 %reduce-scatter.24.cloned.1.call-done = bf16[512,3072]{1,0:T(8,128)(2,1)} async-done(((bf16[1024,3072]{1,0:T(8,128)(2,1)}), bf16[512,3072]{1,0:T(8,128)(2,1)}) %reduce-scatter.24.cloned.1.call-update) | async-done | bytes 3145744 | tf_op jit(solution)/shard_map/reduce_scatter | solution.py:203
  851.2 79.9 %reduce-scatter.26.cloned.1.call-done = bf16[1536,1024]{1,0:T(8,128)(2,1)} async-done(((bf16[3072,1024]{1,0:T(8,128)(2,1)}), bf16[1536,1024]{1,0:T(8,128)(2,1)}) %reduce-scatter.26.cloned.1.call-update) | async-done | bytes 3145744 | tf_op jit(solution)/shard_map/reduce_scatter | solution.py:204
  940.7 41.4 %all-reduce = (f32[1024]{0:T(1024)}, f32[1024]{0:T(1024)}, f32[128]{0:T(128)}, f32[128]{0:T(128)}) all-reduce(f32[1024]{0:T(1024)S(1)} %get-tuple-element.17, f32[1024]{0:T(1024)S(1)} %copy-done.49, f32[128]{0:T(128)S(1)} %bitcast_reduce_fusion, f32[128]{0:T(128)S(1)} %copy-done.56), channel_id=1, replica_groups=mesh['replica'=16,'fsdp'=2] {'replica','fsdp'}, use_global_device_ids=true, to_apply=%region_28.29 | all-reduce | flops 2304 | bytes 18432 | tf_op jit(solution)/shard_map/psum | solution.py:258
  983.1 235.2 %all-reduce.4.cloned.1.call-done = (bf16[512,2048]{1,0:T(8,128)(2,1)}, bf16[512,1024]{1,0:T(8,128)(2,1)}, bf16[512,1024]{1,0:T(8,128)(2,1)}, bf16[1024,1024]{1,0...) async-done(((bf16[512,2048]{1,0:T(8,128)(2,1)}, bf16[512,1024]{1,0:T(8,128)(2,1)}, bf16[512,1024]{1,0:T(8,128)(2,1)}, ...) | async-done | bytes 15728656 | tf_op jit(solution)/shard_map/psum | solution.py:262
  1218.3 5.5 convert_element_type.144
  (239 shorter events, 127.0 us)
Async XLA Ops:
  7.2 38.2 %all-gather.10.cloned.1.call-start = ((), (), s32[]{:S(2)}) async-start(), calls=%async_computation.10 | async-start | bytes 3145728 | tf_op jit(solution)/shard_map/all_gather | solution.py:65
  7.9 72.1 %all-gather.8.cloned.1.call-start = ((), (), s32[]{:S(2)}) async-start(), calls=%async_computation.9 | async-start | bytes 3145728 | tf_op jit(solution)/shard_map/all_gather | solution.py:66
  8.7 135.3 %all-gather.12.cloned.1.call-start = ((), (), s32[]{:S(2)}) async-start(), calls=%async_computation.11 | async-start | bytes 6291456 | tf_op jit(solution)/shard_map/all_gather | solution.py:64
  9.4 192.7 %all-gather.14.cloned.1.call-start = ((), (), s32[]{:S(2)}) async-start(), calls=%async_computation.12 | async-start | bytes 6291456 | tf_op jit(solution)/shard_map/all_gather | solution.py:67
  10.0 273.9 %all-gather.16.cloned.1.call-start = ((), (), s32[]{:S(2)}) async-start(), calls=%async_computation.13 | async-start | bytes 9437184 | tf_op jit(solution)/shard_map/all_gather | solution.py:73
  10.6 355.1 %all-gather.18.cloned.1.call-start = ((), (), s32[]{:S(2)}) async-start(), calls=%async_computation.14 | async-start | bytes 9437184 | tf_op jit(solution)/shard_map/all_gather | solution.py:74
  11.2 34.2 %copy-start.40 = (f32[1024]{0:T(1024)S(1)}, f32[1024]{0:T(1024)}, u32[]{:S(2)}) copy-start(f32[1024]{0:T(1024)} %param.23) | copy-start | bytes 12292
  11.2 436.4 %all-gather.20.cloned.1.call-start = ((), (), s32[]{:S(2)}) async-start(), calls=%async_computation.15 | async-start | bytes 9437184 | tf_op jit(solution)/shard_map/all_gather | solution.py:75
  11.9 478.7 %reduce-scatter.12.cloned.1.call-start = ((), (), s32[]{:S(2)}) async-start(), calls=%async_computation.16 | async-start | bytes 786432 | tf_op jit(solution)/shard_map/reduce_scatter | solution.py:217
  12.2 131.7 %copy-start.44 = (f32[128]{0:T(128)}, f32[128]{0:T(128)S(1)}, u32[]{:S(2)}) copy-start(f32[128]{0:T(128)S(1)} %add_rsqrt_fusion.3) | copy-start | bytes 1540
  13.3 69.4 %copy-start.37 = (f32[128,128]{1,0:T(8,128)}, f32[128,128]{1,0:T(8,128)S(1)}, u32[]{:S(2)}) copy-start(f32[128,128]{1,0:T(8,128)S(1)} %copy.156) | copy-start | bytes 196612
  13.4 69.3 %copy-start.39 = (f32[128,128]{1,0:T(8,128)}, f32[128,128]{1,0:T(8,128)S(1)}, u32[]{:S(2)}) copy-start(f32[128,128]{1,0:T(8,128)S(1)} %copy.157) | copy-start | bytes 196612
  47.5 35.3 %copy-start.2 = (f32[128,1024]{1,0:T(8,128)}, f32[128,1024]{1,0:T(8,128)S(1)}, u32[]{:S(2)}) copy-start(f32[128,1024]{1,0:T(8,128)S(1)} %fusion.71) | copy-start | bytes 1572868
  47.6 34.7 %copy-start.50 = (f32[128]{0:T(128)S(1)}, f32[128]{0:T(128)}, u32[]{:S(2)}) copy-start(f32[128]{0:T(128)} %param.26) | copy-start | bytes 1540
  475.9 32.3 %reduce-scatter.28.cloned.1.call-start = ((), (), s32[]{:S(2)}) async-start(), calls=%async_computation.24 | async-start | bytes 786432 | tf_op jit(solution)/shard_map/reshape | solution.py:238
  480.4 77.3 %reduce-scatter.16.cloned.1.call-start = ((), (), s32[]{:S(2)}) async-start(), calls=%async_computation.18 | async-start | bytes 3145728 | tf_op jit(solution)/shard_map/reduce_scatter | solution.py:247
  495.7 12.4 copy-start.45
  498.9 78.1 %reduce-scatter.18.cloned.1.call-start = ((), (), s32[]{:S(2)}) async-start(), calls=%async_computation.19 | async-start | bytes 3145728 | tf_op jit(solution)/shard_map/reduce_scatter | solution.py:248
  511.3 122.9 %reduce-scatter.14.cloned.1.call-start = ((), (), s32[]{:S(2)}) async-start(), calls=%async_computation.17 | async-start | bytes 6291456 | tf_op jit(solution)/shard_map/reduce_scatter | solution.py:246
  535.9 155.5 %reduce-scatter.20.cloned.1.call-start = ((), (), s32[]{:S(2)}) async-start(), calls=%async_computation.20 | async-start | bytes 6291456 | tf_op jit(solution)/shard_map/reduce_scatter | solution.py:249
  540.4 230.9 %reduce-scatter.22.cloned.1.call-start = ((), (), s32[]{:S(2)}) async-start(), calls=%async_computation.21 | async-start | bytes 9437184 | tf_op jit(solution)/shard_map/reduce_scatter | solution.py:202
  546.1 305.1 %reduce-scatter.24.cloned.1.call-start = ((), (), s32[]{:S(2)}) async-start(), calls=%async_computation.22 | async-start | bytes 9437184 | tf_op jit(solution)/shard_map/reduce_scatter | solution.py:203
  551.9 379.2 %reduce-scatter.26.cloned.1.call-start = ((), (), s32[]{:S(2)}) async-start(), calls=%async_computation.23 | async-start | bytes 9437184 | tf_op jit(solution)/shard_map/reduce_scatter | solution.py:204
  557.6 660.7 %all-reduce.4.cloned.1.call-start = ((), (), s32[]{:S(2)}) async-start(), calls=%async_computation.25 | async-start | bytes 31457280 | tf_op jit(solution)/shard_map/psum | solution.py:262
  (52 other events, 124.9 us)
Sparse Core Ops, SparseCore 0:
  9.5 35.8 all-gather.9
  46.9 33.0 all-gather.7
  81.6 62.3 all-gather.11
  145.4 56.7 all-gather.13
  203.5 80.3 all-gather.15
  285.3 80.3 all-gather.17
  367.2 80.3 all-gather.19
  476.0 14.6 reduce-scatter.11
  493.5 14.6 reduce-scatter.27
  510.8 31.9 reduce-scatter.15
  545.1 31.8 reduce-scatter.17
  579.7 54.3 reduce-scatter.13
  637.0 54.3 reduce-scatter.19
  694.1 77.1 reduce-scatter.21
  774.0 77.1 reduce-scatter.23
  853.9 77.1 reduce-scatter.25
  936.5 281.7 all-reduce.3
where the time goes:
time: 1250 us
  waiting for transfers between devices  1010 us (81%)
  matrix products  88.1 us (7%)
  blocking collectives  65.3 us (5%)
  other arithmetic  34.1 us (3%)
  local copies, waits for them, and re-layouts  27.6 us (2%)
  between operations  14.8 us (1%)
    psum x1, waiting for transfers between devices, shards(): lax.psum(attn_shards[0].astype(jnp.bfloat16), 'replica').astype(jnp.float32)  235 us
    reduce_scatter x1, waiting for transfers between devices, shards(): lax.psum_scatter(grad_up, 'fsdp', scatter_dimension=0, tiled=True)  79.9 us
    reduce_scatter x1, waiting for transfers between devices, shards(): lax.psum_scatter(grad_down, 'fsdp', scatter_dimension=0, tiled=True)  79.9 us
    reduce_scatter x1, waiting for transfers between devices, shards(): lax.psum_scatter(grad_gate, 'fsdp', scatter_dimension=0, tiled=True)  79.9 us
    all_gather x1, waiting for transfers between devices, mlp_weights(): lax.all_gather(w_gate, 'fsdp', axis=0, tiled=True)  77 us
    all_gather x1, waiting for transfers between devices, mlp_weights(): lax.all_gather(w_down, 'fsdp', axis=0, tiled=True)  76.9 us
    all_gather x1, waiting for transfers between devices, mlp_weights(): lax.all_gather(w_up, 'fsdp', axis=0, tiled=True)  76.8 us
    reduce_scatter x1, waiting for transfers between devices, shards(): lax.psum_scatter(grad_out, 'fsdp', scatter_dimension=0, tiled=True)  57.3 us
  transfers between devices with their start and end apart: 17, of which 16 were waited for; matrix products, arithmetic and copies ran while one was open for 7% of the time, Pallas kernels for 0%

commit v1 on v0

--- a/solution.py
+++ b/solution.py
@@ -259,7 +259,9 @@
         (grad_attn_gain, grad_mlp_gain, grad_query_gain, grad_key_gain), ("replica", "fsdp")
     )
     totals = (
-        lax.psum(attn_shards[0].astype(jnp.bfloat16), "replica").astype(jnp.float32),
+        jnp.sum(lax.all_gather(attn_shards[0].astype(jnp.bfloat16), "replica"), axis=0).astype(
+            jnp.float32
+        ),
         lax.psum(attn_shards[1].astype(jnp.bfloat16), "replica").astype(jnp.float32),
         lax.psum(attn_shards[2].astype(jnp.bfloat16), "replica").astype(jnp.float32),
         lax.psum(attn_shards[3].astype(jnp.bfloat16), "replica").astype(jnp.float32),

time: 1250 us -> 1380 us (1.10)
  waiting for transfers between devices: 1010 us -> 1130 us
    all_gather x0 -> x1, waiting for transfers between devices: none -> 150 us  [shards(): lax.all_gather(attn_shards[0].astype(jnp.bfloat16), 'replica')]
    psum x1, waiting for transfers between devices: 235 us -> 205 us  [shards(): lax.psum(attn_shards[1].astype(jnp.bfloat16), 'replica').astype(jnp.float32)]
  transfers between devices with their start and end apart: 17 -> 18, of which waited for: 16 -> 17; matrix products, arithmetic and copies ran while one was open for 7% -> 8% of each run, Pallas kernels for 0% -> 0%
where the time goes in v1:
time: 1380 us
  waiting for transfers between devices  1130 us (82%)
  matrix products  93.3 us (7%)
  blocking collectives  65.4 us (5%)
  other arithmetic  45.1 us (3%)
  local copies, waits for them, and re-layouts  24.2 us (2%)
  between operations  15.2 us (1%)
    psum x1, waiting for transfers between devices, shards(): lax.psum(attn_shards[1].astype(jnp.bfloat16), 'replica').astype(jnp.float32)  205 us
    all_gather x1, waiting for transfers between devices, shards(): lax.all_gather(attn_shards[0].astype(jnp.bfloat16), 'replica')  150 us
    reduce_scatter x1, waiting for transfers between devices, shards(): lax.psum_scatter(grad_gate, 'fsdp', scatter_dimension=0, tiled=True)  80 us
    reduce_scatter x1, waiting for transfers between devices, shards(): lax.psum_scatter(grad_up, 'fsdp', scatter_dimension=0, tiled=True)  79.9 us
    reduce_scatter x1, waiting for transfers between devices, shards(): lax.psum_scatter(grad_down, 'fsdp', scatter_dimension=0, tiled=True)  79.9 us
    all_gather x1, waiting for transfers between devices, mlp_weights(): lax.all_gather(w_gate, 'fsdp', axis=0, tiled=True)  76.9 us
    all_gather x1, waiting for transfers between devices, mlp_weights(): lax.all_gather(w_down, 'fsdp', axis=0, tiled=True)  76.9 us
    all_gather x1, waiting for transfers between devices, mlp_weights(): lax.all_gather(w_up, 'fsdp', axis=0, tiled=True)  76.8 us
  transfers between devices with their start and end apart: 18, of which 17 were waited for; matrix products, arithmetic and copies ran while one was open for 8% of the time, Pallas kernels for 0%

profile of v1, /device:TPU:0, one launch (start us, length us, event | category | flops | bytes accessed | tf_op | source)
XLA Modules:
  0.0 1378.4 jit_solution(2345093331046856226)
XLA Ops:
  13.5 31.9 %all-gather.10.cloned.1.call-done = bf16[1024,1024]{1,0:T(8,128)(2,1)} async-done(((bf16[512,1024]{1,0:T(8,128)(2,1)}), bf16[1024,1024]{1,0:T(8,128)(2,1)}) %all-gather.10.cloned.1.call-update) | async-done | bytes 2097168 | tf_op jit(solution)/shard_map/all_gather | solution.py:66
  47.7 32.4 %all-gather.12.cloned.1.call-done = bf16[1024,1024]{1,0:T(8,128)(2,1)} async-done(((bf16[512,1024]{1,0:T(8,128)(2,1)}), bf16[1024,1024]{1,0:T(8,128)(2,1)}) %all-gather.12.cloned.1.call-update) | async-done | bytes 2097168 | tf_op jit(solution)/shard_map/all_gather | solution.py:65
  82.5 8.7 all_gather.34
  92.0 15.1 %all_gather.36 = bf16[256,8,128]{2,0,1:T(8,128)(2,1)} all-gather(bf16[128,8,128]{2,0,1:T(8,128)(2,1)S(1)} %fusion.46), channel_id=1, replica_groups=mesh['replica'=16,'fsdp'=2] {'fsdp'}, dimensions={0}, use_global_device_ids=true | all-gather | bytes 786432 | tf_op jit(solution)/shard_map/all_gather | solution.py:81
  107.1 36.9 %all-gather.14.cloned.1.call-done = bf16[1024,2048]{1,0:T(8,128)(2,1)} async-done(((bf16[512,2048]{1,0:T(8,128)(2,1)}), bf16[1024,2048]{1,0:T(8,128)(2,1)}) %all-gather.14.cloned.1.call-update) | async-done | bytes 4194320 | tf_op jit(solution)/shard_map/all_gather | solution.py:64
  151.7 50.5 %all-gather.16.cloned.1.call-done = bf16[2048,1024]{1,0:T(8,128)(2,1)} async-done(((bf16[1024,1024]{1,0:T(8,128)(2,1)}), bf16[2048,1024]{1,0:T(8,128)(2,1)}) %all-gather.16.cloned.1.call-update) | async-done | bytes 4194320 | tf_op jit(solution)/shard_map/all_gather | solution.py:67
  207.0 76.9 %all-gather.18.cloned.1.call-done = bf16[1024,3072]{1,0:T(8,128)(2,1)} async-done(((bf16[512,3072]{1,0:T(8,128)(2,1)}), bf16[1024,3072]{1,0:T(8,128)(2,1)}) %all-gather.18.cloned.1.call-update) | async-done | bytes 6291472 | tf_op jit(solution)/shard_map/all_gather | solution.py:73
  288.9 76.8 %all-gather.20.cloned.1.call-done = bf16[1024,3072]{1,0:T(8,128)(2,1)} async-done(((bf16[512,3072]{1,0:T(8,128)(2,1)}), bf16[1024,3072]{1,0:T(8,128)(2,1)}) %all-gather.20.cloned.1.call-update) | async-done | bytes 6291472 | tf_op jit(solution)/shard_map/all_gather | solution.py:74
  370.7 76.9 %all-gather.22.cloned.1.call-done = bf16[3072,1024]{1,0:T(8,128)(2,1)} async-done(((bf16[1536,1024]{1,0:T(8,128)(2,1)}), bf16[3072,1024]{1,0:T(8,128)(2,1)}) %all-gather.22.cloned.1.call-update) | async-done | bytes 6291472 | tf_op jit(solution)/shard_map/all_gather | solution.py:75
  447.6 7.2 multiply_convert_fusion
  480.9 10.3 reduce-scatter.12.cloned.1.call-done
  499.4 9.3 reduce-scatter.28.cloned.1.call-done
  516.3 6.0 fusion.83
  522.4 5.7 fusion.84
  558.9 18.6 %reduce-scatter.18.cloned.1.call-done = bf16[512,1024]{1,0:T(8,128)(2,1)} async-done(((bf16[1024,1024]{1,0:T(8,128)(2,1)}), bf16[512,1024]{1,0:T(8,128)(2,1)}) %reduce-scatter.18.cloned.1.call-update) | async-done | bytes 1048592 | tf_op jit(solution)/shard_map/reduce_scatter | solution.py:248
  577.4 57.1 %reduce-scatter.20.cloned.1.call-done = bf16[1024,1024]{1,0:T(8,128)(2,1)} async-done(((bf16[2048,1024]{1,0:T(8,128)(2,1)}), bf16[1024,1024]{1,0:T(8,128)(2,1)}) %reduce-scatter.20.cloned.1.call-update) | async-done | bytes 2097168 | tf_op jit(solution)/shard_map/reduce_scatter | solution.py:249
  634.6 80.0 %reduce-scatter.22.cloned.1.call-done = bf16[512,3072]{1,0:T(8,128)(2,1)} async-done(((bf16[1024,3072]{1,0:T(8,128)(2,1)}), bf16[512,3072]{1,0:T(8,128)(2,1)}) %reduce-scatter.22.cloned.1.call-update) | async-done | bytes 3145744 | tf_op jit(solution)/shard_map/reduce_scatter | solution.py:202
  714.6 79.9 %reduce-scatter.24.cloned.1.call-done = bf16[512,3072]{1,0:T(8,128)(2,1)} async-done(((bf16[1024,3072]{1,0:T(8,128)(2,1)}), bf16[512,3072]{1,0:T(8,128)(2,1)}) %reduce-scatter.24.cloned.1.call-update) | async-done | bytes 3145744 | tf_op jit(solution)/shard_map/reduce_scatter | solution.py:203
  794.5 79.9 %reduce-scatter.26.cloned.1.call-done = bf16[1536,1024]{1,0:T(8,128)(2,1)} async-done(((bf16[3072,1024]{1,0:T(8,128)(2,1)}), bf16[1536,1024]{1,0:T(8,128)(2,1)}) %reduce-scatter.26.cloned.1.call-update) | async-done | bytes 3145744 | tf_op jit(solution)/shard_map/reduce_scatter | solution.py:204
  874.5 57.0 %reduce-scatter.14.cloned.1.call-done = bf16[512,2048]{1,0:T(8,128)(2,1)} async-done(((bf16[1024,2048]{1,0:T(8,128)(2,1)}), bf16[512,2048]{1,0:T(8,128)(2,1)}) %reduce-scatter.14.cloned.1.call-update) | async-done | bytes 2097168 | tf_op jit(solution)/shard_map/reduce_scatter | solution.py:246
  940.2 41.6 %all-reduce = (f32[1024]{0:T(1024)}, f32[1024]{0:T(1024)}, f32[128]{0:T(128)}, f32[128]{0:T(128)}) all-reduce(f32[1024]{0:T(1024)S(1)} %get-tuple-element.17, f32[1024]{0:T(1024)S(1)} %copy-done.44, f32[128]{0:T(128)S(1)} %bitcast_reduce_fusion, f32[128]{0:T(128)S(1)} %copy-done.51), channel_id=1, replica_groups=mesh['replica'=16,'fsdp'=2] {'replica','fsdp'}, use_global_device_ids=true, to_apply=%region_28.29 | all-reduce | flops 2304 | bytes 18432 | tf_op jit(solution)/shard_map/psum | solution.py:258
  982.8 205.2 %all-reduce.4.cloned.1.call-done = (bf16[512,1024]{1,0:T(8,128)(2,1)}, bf16[512,1024]{1,0:T(8,128)(2,1)}, bf16[1024,1024]{1,0:T(8,128)(2,1)}, bf16[512,3072]{1,0...) async-done(((bf16[512,1024]{1,0:T(8,128)(2,1)}, bf16[512,1024]{1,0:T(8,128)(2,1)}, bf16[1024,1024]{1,0:T(8,128)(2,1)}, bf16[512,3072]{1,0:T(8,128)(2,1)}, ...) | async-done | bytes 13631504 | tf_op jit(solution)/shard_map/psum | solution.py:265
  1206.7 150.3 %all-gather.24.cloned.1.call-done = bf16[8192,2048]{1,0:T(8,128)(2,1)} async-done(((bf16[512,2048]{1,0:T(8,128)(2,1)}), bf16[8192,2048]{1,0:T(8,128)(2,1)}) %all-gather.24.cloned.1.call-update) | async-done | bytes 33554448 | tf_op jit(solution)/shard_map/all_gather | solution.py:262
  1357.0 11.7 reduce_sum.155
  (233 shorter events, 137.4 us)
Async XLA Ops:
  7.2 38.2 %all-gather.10.cloned.1.call-start = ((), (), s32[]{:S(2)}) async-start(), calls=%async_computation.9 | async-start | bytes 3145728 | tf_op jit(solution)/shard_map/all_gather | solution.py:66
  7.9 72.1 %all-gather.12.cloned.1.call-start = ((), (), s32[]{:S(2)}) async-start(), calls=%async_computation.10 | async-start | bytes 3145728 | tf_op jit(solution)/shard_map/all_gather | solution.py:65
  8.7 135.3 %all-gather.14.cloned.1.call-start = ((), (), s32[]{:S(2)}) async-start(), calls=%async_computation.11 | async-start | bytes 6291456 | tf_op jit(solution)/shard_map/all_gather | solution.py:64
  9.4 192.7 %all-gather.16.cloned.1.call-start = ((), (), s32[]{:S(2)}) async-start(), calls=%async_computation.12 | async-start | bytes 6291456 | tf_op jit(solution)/shard_map/all_gather | solution.py:67
  10.0 273.9 %all-gather.18.cloned.1.call-start = ((), (), s32[]{:S(2)}) async-start(), calls=%async_computation.13 | async-start | bytes 9437184 | tf_op jit(solution)/shard_map/all_gather | solution.py:73
  10.6 355.1 %all-gather.20.cloned.1.call-start = ((), (), s32[]{:S(2)}) async-start(), calls=%async_computation.14 | async-start | bytes 9437184 | tf_op jit(solution)/shard_map/all_gather | solution.py:74
  11.2 436.4 %all-gather.22.cloned.1.call-start = ((), (), s32[]{:S(2)}) async-start(), calls=%async_computation.15 | async-start | bytes 9437184 | tf_op jit(solution)/shard_map/all_gather | solution.py:75
  11.9 479.2 %reduce-scatter.12.cloned.1.call-start = ((), (), s32[]{:S(2)}) async-start(), calls=%async_computation.16 | async-start | bytes 786432 | tf_op jit(solution)/shard_map/reduce_scatter | solution.py:217
  12.2 131.7 %copy-start.39 = (f32[128]{0:T(128)}, f32[128]{0:T(128)S(1)}, u32[]{:S(2)}) copy-start(f32[128]{0:T(128)S(1)} %add_rsqrt_fusion.3) | copy-start | bytes 1540
  13.3 78.3 %copy-start.34 = (f32[128,128]{1,0:T(8,128)}, f32[128,128]{1,0:T(8,128)S(1)}, u32[]{:S(2)}) copy-start(f32[128,128]{1,0:T(8,128)S(1)} %copy.157) | copy-start | bytes 196612
  13.4 78.2 %copy-start.32 = (f32[128,128]{1,0:T(8,128)}, f32[128,128]{1,0:T(8,128)S(1)}, u32[]{:S(2)}) copy-start(f32[128,128]{1,0:T(8,128)S(1)} %copy.156) | copy-start | bytes 196612
  47.6 43.5 %copy-start.45 = (f32[128]{0:T(128)S(1)}, f32[128]{0:T(128)}, u32[]{:S(2)}) copy-start(f32[128]{0:T(128)} %param.26) | copy-start | bytes 1540
  476.4 32.3 %reduce-scatter.28.cloned.1.call-start = ((), (), s32[]{:S(2)}) async-start(), calls=%async_computation.25 | async-start | bytes 786432 | tf_op jit(solution)/shard_map/reshape | solution.py:238
  480.8 78.1 %reduce-scatter.16.cloned.1.call-start = ((), (), s32[]{:S(2)}) async-start(), calls=%async_computation.18 | async-start | bytes 3145728 | tf_op jit(solution)/shard_map/reduce_scatter | solution.py:247
  499.3 78.1 %reduce-scatter.18.cloned.1.call-start = ((), (), s32[]{:S(2)}) async-start(), calls=%async_computation.19 | async-start | bytes 3145728 | tf_op jit(solution)/shard_map/reduce_scatter | solution.py:248
  511.7 122.9 %reduce-scatter.20.cloned.1.call-start = ((), (), s32[]{:S(2)}) async-start(), calls=%async_computation.20 | async-start | bytes 6291456 | tf_op jit(solution)/shard_map/reduce_scatter | solution.py:249
  516.2 198.4 %reduce-scatter.22.cloned.1.call-start = ((), (), s32[]{:S(2)}) async-start(), calls=%async_computation.21 | async-start | bytes 9437184 | tf_op jit(solution)/shard_map/reduce_scatter | solution.py:202
  522.3 272.2 %reduce-scatter.24.cloned.1.call-start = ((), (), s32[]{:S(2)}) async-start(), calls=%async_computation.22 | async-start | bytes 9437184 | tf_op jit(solution)/shard_map/reduce_scatter | solution.py:203
  528.1 346.3 %reduce-scatter.26.cloned.1.call-start = ((), (), s32[]{:S(2)}) async-start(), calls=%async_computation.23 | async-start | bytes 9437184 | tf_op jit(solution)/shard_map/reduce_scatter | solution.py:204
  533.9 397.7 %reduce-scatter.14.cloned.1.call-start = ((), (), s32[]{:S(2)}) async-start(), calls=%async_computation.17 | async-start | bytes 6291456 | tf_op jit(solution)/shard_map/reduce_scatter | solution.py:246
  558.8 629.1 %all-reduce.4.cloned.1.call-start = ((), (), s32[]{:S(2)}) async-start(), calls=%async_computation.26 | async-start | bytes 27262976 | tf_op jit(solution)/shard_map/psum | solution.py:265
  874.5 57.2 %copy-start.8 = (f32[128,1024]{1,0:T(8,128)S(1)}, f32[128,1024]{1,0:T(8,128)}, u32[]{:S(2)}) copy-start(f32[128,1024]{1,0:T(8,128)} %copy-done.6) | copy-start | bytes 1572868
  874.5 57.2 %copy-start.16 = (bf16[128,3072]{1,0:T(8,128)(2,1)S(1)}, bf16[128,3072]{1,0:T(8,128)(2,1)}, u32[]{:S(2)}) copy-start(bf16[128,3072]{1,0:T(8,128)(2,1)} %get-tuple-element.34) | copy-start | bytes 2359300
  874.5 482.5 %all-gather.24.cloned.1.call-start = ((), (), s32[]{:S(2)}) async-start(), calls=%async_computation.24 | async-start | bytes 35651584 | tf_op jit(solution)/shard_map/all_gather | solution.py:262
  (48 other events, 214.6 us)
Sparse Core Ops, SparseCore 0:
  9.5 35.8 all-gather.9
  46.9 33.0 all-gather.11
  81.6 62.3 all-gather.13
  145.4 56.7 all-gather.15
  203.5 80.3 all-gather.17
  285.3 80.3 all-gather.19
  367.2 80.3 all-gather.21
  476.5 14.6 reduce-scatter.11
  494.0 14.6 reduce-scatter.27
  511.3 31.8 reduce-scatter.15
  545.5 31.8 reduce-scatter.17
  580.2 54.3 reduce-scatter.19
  637.4 77.1 reduce-scatter.21
  717.4 77.1 reduce-scatter.23
  797.3 77.1 reduce-scatter.25
  877.1 54.3 reduce-scatter.13
  936.7 251.2 all-reduce.3
  1189.4 167.5 all-gather.23
